TPU v7x, 128 devices: a whole 4x4x4 slice. The times are simulated.
128 devices in a mesh: grp: 4 (over y), col: 32 (over x, z, core).
Axes of the slice: x: 4, y: 4, z: 4, core: 2. Of those that a mesh axis runs over, the one named last changes fastest.
Arguments:
- blocks: bfloat16 [24576, 32, 1024], P(('grp', 'col'))
- i_index: int32 [24576], P(('grp', 'col')), may hold values from 0 to 63
- j_index: int32 [24576], P(('grp', 'col')), may hold values from 0 to 63
- k_index: int32 [24576], P(('grp', 'col')), may hold values from 0 to 15
- block_count: int32 [128], P(('grp', 'col')), may hold values from 24 to 192, as said below
- b_factor: float32 [65536, 256], P(('grp', 'col'))
- c_factor: float32 [16384, 256], P(('grp', 'col'))
Outputs:
- a_update: float32 [8192, 256], P(('grp', 'col'))
- b_update: float32 [65536, 256], P(('grp', 'col'))
Inputs may be any that keep to these rules, and one draw needn't show every extreme that they name: block_count[d] is the number of live slots of device d = 32 * (grp index) + (col index): its slots d * 192 to d * 192 + block_count[d] - 1; every other slot is ignored. Some device has exactly 192 live slots.
All inputs are finite; a program needn't handle non-finite values.
Results may differ from a plain program's by a relative error of at most 0.005.
The roundings to bfloat16 on the way count: a program that leaves them out, or rounds other values in their place, can miss the bound.
Values may be sent and summed in bfloat16 or wider, within the bound.
No kernel may reach another device: no remote copies, remote signals or barrier semaphores. Data moves between devices by JAX's collectives and lax.ppermute only.
A program may use at most 128 MiB of HBM per device.

v0:
```python
import jax
import jax.numpy as jnp
from jax import lax
from jax.sharding import PartitionSpec as P

A_DEV = 2


def solve_rows(gram, right_side):
    factor_low = lax.linalg.cholesky(gram)
    halfway = lax.linalg.triangular_solve(
        factor_low, right_side, left_side=False, lower=True, transpose_a=True
    )
    return lax.linalg.triangular_solve(
        factor_low, halfway, left_side=False, lower=True, transpose_a=False
    )


def mode_term(
    blocks,
    left_rows,
    left_index,
    tail_rows,
    tail_index,
    target_index,
    live_mask,
    targets,
    first_mode,
):
    block_edge = blocks.shape[1]
    rank_width = left_rows.shape[1]
    group_size = 16
    groups = blocks.shape[0] // group_size
    left_table = left_rows.reshape(-1, block_edge, rank_width)
    tail_table = tail_rows.reshape(-1, block_edge, rank_width)
    target_ids = jnp.arange(targets, dtype=jnp.int32)

    def one_step(running, inputs):
        tensor_group, left_idx, tail_idx, target_idx, alive_row = inputs
        left_blk = left_table[left_idx].astype(jnp.float32)
        tail_blk = tail_table[tail_idx].astype(jnp.float32)
        product = (left_blk[:, :, None, :] * tail_blk[:, None, :, :]).astype(jnp.bfloat16)
        if first_mode:
            result = jnp.einsum(
                "bim,bmr->bir",
                tensor_group,
                product.reshape(group_size, block_edge * block_edge, rank_width),
                preferred_element_type=jnp.float32,
            )
        else:
            result = jnp.einsum(
                "bijk,bikr->bjr",
                tensor_group.reshape(group_size, block_edge, block_edge, block_edge),
                product,
                preferred_element_type=jnp.float32,
            )
        select = (target_idx[None, :] == target_ids[:, None]).astype(jnp.float32) * alive_row[
            None, :
        ]
        update = jnp.dot(
            select,
            result.reshape(group_size, block_edge * rank_width),
            precision=lax.Precision.HIGHEST,
        )
        return (running + update, None)

    inputs = (
        blocks.reshape(groups, group_size, block_edge, block_edge * block_edge),
        left_index.reshape(groups, group_size),
        tail_index.reshape(groups, group_size),
        target_index.reshape(groups, group_size),
        live_mask.reshape(groups, group_size),
    )
    start_value = jnp.zeros((targets, block_edge * rank_width), jnp.float32)
    running, _ = lax.scan(one_step, start_value, inputs)
    return running.reshape(targets * block_edge, rank_width)


def on_device(blocks, i_index, j_index, k_index, block_count, b_factor, c_factor):
    highest = lax.Precision.HIGHEST
    block_edge = blocks.shape[1]
    gram_second, gram_third = lax.psum(
        (
            jnp.dot(b_factor.T, b_factor, precision=highest),
            jnp.dot(c_factor.T, c_factor, precision=highest),
        ),
        ("grp", "col"),
    )
    b_range, c_range = (
        lax.all_gather(b_factor.astype(jnp.bfloat16), "grp", axis=0, tiled=True),
        lax.all_gather(c_factor.astype(jnp.bfloat16), "grp", axis=0, tiled=True),
    )
    live_mask = (jnp.arange(blocks.shape[0], dtype=jnp.int32) < block_count[0]).astype(jnp.float32)
    first_targets = A_DEV * lax.axis_size("col")
    second_targets = b_range.shape[0] // block_edge
    partial_value = mode_term(
        blocks, b_range, j_index, c_range, k_index, i_index, live_mask, first_targets, True
    )
    gram_one = gram_second * gram_third
    whole_sum = lax.psum(partial_value, "col")
    a_whole = solve_rows(gram_one, whole_sum)
    gram_first = lax.psum(jnp.dot(a_whole.T, a_whole, precision=highest), "grp")
    col_norm = jnp.sqrt(jnp.diagonal(gram_first) + 1e-06)
    a_range = (a_whole / col_norm[None, :]).astype(jnp.bfloat16)
    own_rows = A_DEV * block_edge
    a_update = lax.dynamic_slice_in_dim(a_whole, lax.axis_index("col") * own_rows, own_rows, 0)
    gram_two = gram_first / (col_norm[:, None] * col_norm[None, :]) * gram_third
    partial_two = mode_term(
        blocks, a_range, i_index, c_range, k_index, j_index, live_mask, second_targets, False
    )
    own_two = lax.psum_scatter(partial_two, "grp", scatter_dimension=0, tiled=True)
    b_update = solve_rows(gram_two, own_two)
    return (a_update, b_update)


def solution(mesh):
    return jax.shard_map(
        on_device,
        mesh=mesh,
        in_specs=(
            P(("grp", "col"), None, None),
            P(("grp", "col")),
            P(("grp", "col")),
            P(("grp", "col")),
            P(("grp", "col")),
            P(("grp", "col"), None),
            P(("grp", "col"), None),
        ),
        out_specs=(P(("grp", "col"), None), P(("grp", "col"), None)),
        check_vma=False,
    )
```

profile of v0, /device:TPU:0, one launch (start us, length us, event | category | flops | bytes accessed | tf_op | source)
XLA Modules:
  0.0 780.1 jit_solution(10742429783290168959)
XLA Ops:
  15.0 13.0 %all_gather.7 = bf16[512,256]{1,0:T(8,128)(2,1)S(1)} all-gather(bf16[128,256]{1,0:T(8,128)(2,1)S(1)} %convert_element_type.56), channel_id=1, replica_groups=mesh['grp'=4,'col'=32] {'grp'}, dimensions={0}, use_global_device_ids=true | all-gather | bytes 327680 | tf_op jit(solution)/shard_map/all_gather | solution.py:91
  28.0 135.6 %all-reduce.10.cloned.1.call-done = (f32[256,256]{0,1:T(8,128)}, f32[256,256]{0,1:T(8,128)}) async-done(((f32[256,256]{0,1:T(8,128)}, f32[256,256]{0,1:T(8,128)}), (f32[256,256]{0,1:T(8,128)}, f32[256,256]{0,1:T(8,128)})) %all-reduce.10.cloned.1.call-update) | async-done | bytes 524304 | tf_op jit(solution)/shard_map/psum | solution.py:82
  164.8 11.7 %custom-call.29 = f32[128,128]{1,0:T(8,128)S(1)} custom-call(f32[128,128]{1,0:T(8,128)S(1)} %slice.101), custom_call_target="Cholesky" | custom-call | tf_op jit(solution)/shard_map/cholesky/custom-call.2 | solution.py:10
  176.6 9.8 %custom-call.30 = f32[1,128,128]{1,2,0:T(8,128)S(1)} custom-call(f32[1,128,128]{2,1,0:T(8,128)S(1)} %get-tuple-element.262), custom_call_target="InvertDiagBlocksLowerTriangular" | custom-call | tf_op jit(solution)/shard_map/cholesky/custom-call.7 | solution.py:10
  187.1 11.7 %custom-call.31 = f32[128,128]{1,0:T(8,128)S(1)} custom-call(f32[128,128]{1,0:T(8,128)S(1)} %convolution_subtract_fusion.5), custom_call_target="Cholesky" | custom-call | tf_op jit(solution)/shard_map/cholesky/custom-call.3 | solution.py:10
  198.9 141.3 %while.26 = (s32[]{:T(128)}, f32[64,8192]{1,0:T(8,128)S(1)}, s32[12,16]{1,0:T(8,128)S(1)}, f32[12,16]{1,0:T(8,128)S(1)}, bf16[12,16,32,1024]{3,2,1,0:T(8,128)(2,...) while((s32[]{:T(128)}, f32[64,8192]{1,0:T(8,128)S(1)}, ...), condition=%wide.region_1.0_spmd.clone, body=%wide.region_0.0_spmd.clone.sunk | while | flops 378802272 | bytes 27796492 | solution.py:75
  348.3 19.7 %custom-call.20 = f32[2,128,128]{1,2,0:T(8,128)S(1)} custom-call(f32[2,128,128]{2,1,0:T(8,128)S(1)} %get-tuple-element.116), custom_call_target="InvertDiagBlocksLowerTriangular" | custom-call | tf_op jit(solution)/shard_map/triangular_solve | solution.py:11
  368.0 80.2 %all-reduce.6.cloned.1.call-done = f32[2048,256]{1,0:T(8,128)} async-done(((f32[2048,256]{1,0:T(8,128)}), f32[2048,256]{1,0:T(8,128)}) %all-reduce.6.cloned.1.call-update) | async-done | bytes 2097168 | tf_op jit(solution)/shard_map/psum | solution.py:100
  461.2 40.8 %all-reduce.8.cloned.1.call-done = f32[256,256]{0,1:T(8,128)} async-done(((f32[256,256]{0,1:T(8,128)}), f32[256,256]{0,1:T(8,128)}) %all-reduce.8.cloned.1.call-update) | async-done | bytes 262160 | tf_op jit(solution)/shard_map/psum | solution.py:102
  507.1 195.0 %while.27 = (s32[]{:T(128)}, f32[64,8192]{1,0:T(8,128)S(1)}, s32[12,16]{1,0:T(8,128)}, f32[12,16]{1,0:T(8,128)}, bf16[12,16,32,1024]{3,2,1,0:T(8,128)(2,1)}, /*i...) while((s32[]{:T(128)}, f32[64,8192]{1,0:T(8,128)S(1)}, ...), condition=%wide.region_11.13_spmd.clone, body=%wide.region_10.12_spmd.clone.sunk | while | flops 378802272 | bytes 15213583 | solution.py:75
  508.4 4.4 reshape.345
  524.7 4.4 reshape.345
  540.9 4.4 reshape.345
  557.2 4.4 reshape.345
  573.4 4.4 reshape.345
  589.7 4.4 reshape.345
  622.2 4.4 reshape.345
  654.7 4.4 reshape.345
  670.9 4.4 reshape.345
  687.2 4.4 reshape.345
  706.2 11.7 %custom-call.32 = f32[128,128]{1,0:T(8,128)S(1)} custom-call(f32[128,128]{1,0:T(8,128)S(1)} %slice.104), custom_call_target="Cholesky" | custom-call | tf_op jit(solution)/shard_map/cholesky/custom-call.2 | solution.py:10
  718.0 9.8 %custom-call.33 = f32[1,128,128]{1,2,0:T(8,128)S(1)} custom-call(f32[1,128,128]{2,1,0:T(8,128)S(1)} %get-tuple-element.258), custom_call_target="InvertDiagBlocksLowerTriangular" | custom-call | tf_op jit(solution)/shard_map/cholesky/custom-call.7 | solution.py:10
  728.5 11.7 %custom-call.34 = f32[128,128]{1,0:T(8,128)S(1)} custom-call(f32[128,128]{1,0:T(8,128)S(1)} %convolution_subtract_fusion.4), custom_call_target="Cholesky" | custom-call | tf_op jit(solution)/shard_map/cholesky/custom-call.3 | solution.py:10
  746.9 19.8 %custom-call.21 = f32[2,128,128]{1,2,0:T(8,128)S(1)} custom-call(f32[2,128,128]{2,1,0:T(8,128)S(1)} %get-tuple-element.124), custom_call_target="InvertDiagBlocksLowerTriangular" | custom-call | tf_op jit(solution)/shard_map/triangular_solve | solution.py:11
  (439 shorter events, 346.4 us)
Async XLA Ops:
  8.0 5.2 copy-start.5
  8.0 6.0 copy-start.8
  8.0 6.0 copy-start.12
  8.0 6.8 copy-start.13
  8.0 6.9 copy-start.14
  8.0 155.5 %all-reduce.10.cloned.1.call-start = ((), (), s32[]{:S(2)}) async-start(), calls=%async_computation.5 | async-start | bytes 1048576 | tf_op jit(solution)/shard_map/psum | solution.py:82
  13.2 185.7 %all-gather.2.cloned.1.call-start = ((), (), s32[]{:S(2)}) async-start(), calls=%async_computation.1 | async-start | bytes 1310720 | tf_op jit(solution)/shard_map/all_gather | solution.py:90
  14.0 434.3 %all-reduce.6.cloned.1.call-start = ((), (), s32[]{:S(2)}) async-start(), calls=%async_computation.2 | async-start | bytes 4194304 | tf_op jit(solution)/shard_map/psum | solution.py:100
  340.2 1.5 copy-start.10
  340.2 1.5 copy-start.11
  341.8 160.2 %all-reduce.8.cloned.1.call-start = ((), (), s32[]{:S(2)}) async-start(), calls=%async_computation.3 | async-start | bytes 524288 | tf_op jit(solution)/shard_map/psum | solution.py:102
  348.3 103.3 %copy-start.7 = (f32[256,256]{1,0:T(8,128)}, f32[256,256]{1,0:T(8,128)S(1)}, u32[]{:S(2)}) copy-start(f32[256,256]{1,0:T(8,128)S(1)} %get-tuple-element.553) | copy-start | bytes 786436
  348.3 103.3 %copy-start.15 = (s32[2,2]{1,0:T(2,128)}, s32[2,2]{1,0:T(2,128)S(1)}, u32[]{:S(2)}) copy-start(s32[2,2]{1,0:T(2,128)S(1)} %get-tuple-element.571) | copy-start | bytes 52
  448.3 2.4 copy-start.6
  453.6 51.0 %copy-start = (f32[2048,128]{1,0:T(8,128)}, f32[2048,128]{1,0:T(8,128)S(1)}, u32[]{:S(2)}) copy-start(f32[2048,128]{1,0:T(8,128)S(1)} %fusion.48) | copy-start | bytes 3145732
  456.5 4.7 copy-start.2
  460.7 306.1 %reduce-scatter.2.cloned.1.call-start = ((), (), s32[]{:S(2)}) async-start(), calls=%async_computation.4 | async-start | bytes 2621440 | tf_op jit(solution)/shard_map/reduce_scatter | solution.py:111
  703.6 1.2 copy-start.1
  703.6 1.5 copy-start.3
  703.6 2.2 copy-start.4
  703.6 2.2 copy-start.9
  706.0 36.9 %copy-start.16 = (s32[2,2]{1,0:T(2,128)S(1)}, s32[2,2]{1,0:T(2,128)}, u32[]{:S(2)}) copy-start(s32[2,2]{1,0:T(2,128)} %copy-done.15) | copy-start | bytes 52
Sparse Core Ops, SparseCore 0:
  13.8 149.6 all-reduce.9
Sparse Core Ops, SparseCore 1:
  15.9 26.6 all-gather.1
  341.9 106.3 all-reduce.5
  460.8 41.2 all-reduce.7
  703.7 30.0 reduce-scatter.1
where the time goes:
time: 792 us; the launch traced here: 780 us
  waiting for transfers between devices  257 us (32%)
  local copies, waits for them, and re-layouts  166 us (21%)
  other arithmetic  162 us (20%)
  matrix products  159 us (20%)
  between operations  19.7 us (2%)
  blocking collectives  13 us (2%)
    psum x1, waiting for transfers between devices, on_device(): lax.psum((jnp.dot(b_factor.T, b_factor, precision=highest), jnp.dot(c_fac...  136 us
    psum x1, waiting for transfers between devices, on_device(): whole_sum = lax.psum(partial_value, 'col')  80.2 us
    another operation x13, other arithmetic, solve_rows(): factor_low = lax.linalg.cholesky(gram)  68.6 us
    dot_general x24, matrix products, one_step(): jnp.dot(select, result.reshape(group_size, block_edge * rank_width), prec...  55 us
    reshape x12, local copies, waits for them, and re-layouts, one_step(): tensor_group.reshape(group_size, block_edge, block_edge, block_edge)  52.3 us
    dot_general x12, matrix products, one_step(): jnp.einsum('bijk,bikr->bjr', tensor_group.reshape(group_size, block_edge,...  48.5 us
    convert_element_type x12, other arithmetic, one_step(): (left_blk[:, :, None, :] * tail_blk[:, None, :, :]).astype(jnp.bfloat16)  46.2 us
    gather x24, local copies, waits for them, and re-layouts, one_step(): left_blk = left_table[left_idx].astype(jnp.float32)  42.9 us
  transfers between devices with their start and end apart: 5, of which 3 were waited for; matrix products, arithmetic and copies ran while one was open for 15% of the time, Pallas kernels for 0%

commit v1 on v0

--- a/solution.py
+++ b/solution.py
@@ -80,11 +80,14 @@
     highest = lax.Precision.HIGHEST
     block_edge = blocks.shape[1]
     gram_second, gram_third = lax.psum(
-        (
-            jnp.dot(b_factor.T, b_factor, precision=highest),
-            jnp.dot(c_factor.T, c_factor, precision=highest),
+        lax.psum(
+            (
+                jnp.dot(b_factor.T, b_factor, precision=highest),
+                jnp.dot(c_factor.T, c_factor, precision=highest),
+            ),
+            "col",
         ),
-        ("grp", "col"),
+        "grp",
     )
     b_range, c_range = (
         lax.all_gather(b_factor.astype(jnp.bfloat16), "grp", axis=0, tiled=True),

time: 792 us -> 757 us (0.956)
  waiting for transfers between devices: 257 us -> 204 us
  other arithmetic: 162 us -> 183 us
    psum x1, waiting for transfers between devices: 136 us -> 44.8 us  [on_device(): lax.psum(lax.psum((jnp.dot(b_factor.T, b_factor, precision=highest), jnp....]
    psum x1, waiting for transfers between devices: 80.2 us -> 110 us  [on_device(): whole_sum = lax.psum(partial_value, 'col')]
    convert_element_type x24, other arithmetic: 0.97 us -> 10.6 us  [one_step(): tail_blk = tail_table[tail_idx].astype(jnp.float32)]
    convert_element_type x24, other arithmetic: 0.97 us -> 10.5 us  [one_step(): left_blk = left_table[left_idx].astype(jnp.float32)]
  transfers between devices with their start and end apart: 5 -> 5, of which waited for: 3 -> 4; matrix products, arithmetic and copies ran while one was open for 15% -> 9% of each run, Pallas kernels for 0% -> 0%
where the time goes in v1:
time: 757 us; the launch traced here: 748 us
  waiting for transfers between devices  204 us (27%)
  other arithmetic  183 us (24%)
  local copies, waits for them, and re-layouts  169 us (22%)
  matrix products  158 us (21%)
  between operations  17.7 us (2%)
  blocking collectives  12.9 us (2%)
    psum x1, waiting for transfers between devices, on_device(): whole_sum = lax.psum(partial_value, 'col')  110 us
    another operation x13, other arithmetic, solve_rows(): factor_low = lax.linalg.cholesky(gram)  68.6 us
    dot_general x24, matrix products, one_step(): jnp.dot(select, result.reshape(group_size, block_edge * rank_width), prec...  54.9 us
    reshape x12, local copies, waits for them, and re-layouts, one_step(): tensor_group.reshape(group_size, block_edge, block_edge, block_edge)  52.4 us
    dot_general x12, matrix products, one_step(): jnp.einsum('bijk,bikr->bjr', tensor_group.reshape(group_size, block_edge,...  51.2 us
    convert_element_type x12, other arithmetic, one_step(): (left_blk[:, :, None, :] * tail_blk[:, None, :, :]).astype(jnp.bfloat16)  46.2 us
    psum x1, waiting for transfers between devices, on_device(): lax.psum(lax.psum((jnp.dot(b_factor.T, b_factor, precision=highest), jnp....  44.8 us
    gather x24, local copies, waits for them, and re-layouts, one_step(): left_blk = left_table[left_idx].astype(jnp.float32)  42.9 us
  transfers between devices with their start and end apart: 5, of which 4 were waited for; matrix products, arithmetic and copies ran while one was open for 9% of the time, Pallas kernels for 0%

profile of v1, /device:TPU:0, one launch (start us, length us, event | category | flops | bytes accessed | tf_op | source)
XLA Modules:
  0.0 748.2 jit_solution(8097626388034483962)
XLA Ops:
  13.0 12.9 %all_gather.7 = bf16[512,256]{1,0:T(8,128)(2,1)S(1)} all-gather(bf16[128,256]{1,0:T(8,128)(2,1)S(1)} %convert_element_type.56), channel_id=1, replica_groups=mesh['grp'=4,'col'=32] {'grp'}, dimensions={0}, use_global_device_ids=true | all-gather | bytes 327680 | tf_op jit(solution)/shard_map/all_gather | solution.py:94
  29.6 7.1 all-gather.2.cloned.1.call-done
  36.7 141.0 %while.26 = (s32[]{:T(128)}, f32[64,8192]{1,0:T(8,128)S(1)}, s32[12,16]{1,0:T(8,128)S(1)}, f32[12,16]{1,0:T(8,128)S(1)}, bf16[12,16,32,1024]{3,2,1,0:T(8,128)(2,...) while((s32[]{:T(128)}, f32[64,8192]{1,0:T(8,128)S(1)}, ...), condition=%wide.region_1.0_spmd.clone, body=%wide.region_0.0_spmd.clone.sunk | while | flops 378802272 | bytes 27796992 | solution.py:75
  179.4 109.9 %all-reduce.9.cloned.1.call-done = (f32[2048,256]{1,0:T(8,128)}, f32[256,256]{0,1:T(8,128)}, f32[256,256]{0,1:T(8,128)}) async-done(((f32[2048,256]{1,0:T(8,128)}, f32[256,256]{0,1:T(8,128)}, f32[256,256]{0,1:T(8,128)}), (f32[2048,256]{1,0:T(8,128)}, f32[256,256]{0,1:T(8,128)}, f32[256,256]{0,1:T(8,128)})) %all-reduce.9.cloned.1.call-update) | async-done | bytes 2621456 | tf_op jit(solution)/shard_map/psum | solution.py:103
  289.5 44.8 %all-reduce.11.cloned.1.call-done = (f32[256,256]{0,1:T(8,128)}, f32[256,256]{0,1:T(8,128)}) async-done(((f32[256,256]{0,1:T(8,128)}, f32[256,256]{0,1:T(8,128)}), (f32[256,256]{0,1:T(8,128)}, f32[256,256]{0,1:T(8,128)})) %all-reduce.11.cloned.1.call-update) | async-done | bytes 524304 | tf_op jit(solution)/shard_map/psum | solution.py:82
  335.6 11.7 %custom-call.29 = f32[128,128]{1,0:T(8,128)S(1)} custom-call(f32[128,128]{1,0:T(8,128)S(1)} %slice.101), custom_call_target="Cholesky" | custom-call | tf_op jit(solution)/shard_map/cholesky/custom-call.2 | solution.py:10
  347.4 9.8 %custom-call.30 = f32[1,128,128]{1,2,0:T(8,128)S(1)} custom-call(f32[1,128,128]{2,1,0:T(8,128)S(1)} %get-tuple-element.265), custom_call_target="InvertDiagBlocksLowerTriangular" | custom-call | tf_op jit(solution)/shard_map/cholesky/custom-call.7 | solution.py:10
  357.9 11.7 %custom-call.31 = f32[128,128]{1,0:T(8,128)S(1)} custom-call(f32[128,128]{1,0:T(8,128)S(1)} %convolution_subtract_fusion.5), custom_call_target="Cholesky" | custom-call | tf_op jit(solution)/shard_map/cholesky/custom-call.3 | solution.py:10
  371.9 4.7 while.24
  376.6 19.7 %custom-call.20 = f32[2,128,128]{1,2,0:T(8,128)S(1)} custom-call(f32[2,128,128]{2,1,0:T(8,128)S(1)} %get-tuple-element.116), custom_call_target="InvertDiagBlocksLowerTriangular" | custom-call | tf_op jit(solution)/shard_map/triangular_solve | solution.py:11
  407.7 42.2 %all-reduce.7.cloned.1.call-done = f32[256,256]{0,1:T(8,128)} async-done(((f32[256,256]{0,1:T(8,128)}), f32[256,256]{0,1:T(8,128)}) %all-reduce.7.cloned.1.call-update) | async-done | bytes 262160 | tf_op jit(solution)/shard_map/psum | solution.py:105
  455.0 216.3 %while.27 = (s32[]{:T(128)}, f32[64,8192]{1,0:T(8,128)S(1)}, s32[12,16]{1,0:T(8,128)}, f32[12,16]{1,0:T(8,128)}, bf16[12,16,32,1024]{3,2,1,0:T(8,128)(2,1)}, /*i...) while((s32[]{:T(128)}, f32[64,8192]{1,0:T(8,128)S(1)}, ...), condition=%wide.region_13.15_spmd.clone, body=%wide.region_12.14_spmd.clone.sunk | while | flops 378802272 | bytes 15213575 | solution.py:75
  460.4 4.4 reshape.345
  478.4 4.4 reshape.345
  496.5 4.4 reshape.345
  514.5 4.4 reshape.345
  532.5 4.4 reshape.345
  550.6 4.4 reshape.345
  568.6 4.4 reshape.345
  604.6 4.4 reshape.345
  675.5 11.7 %custom-call.32 = f32[128,128]{1,0:T(8,128)S(1)} custom-call(f32[128,128]{1,0:T(8,128)S(1)} %slice.104), custom_call_target="Cholesky" | custom-call | tf_op jit(solution)/shard_map/cholesky/custom-call.2 | solution.py:10
  687.3 9.8 %custom-call.33 = f32[1,128,128]{1,2,0:T(8,128)S(1)} custom-call(f32[1,128,128]{2,1,0:T(8,128)S(1)} %get-tuple-element.261), custom_call_target="InvertDiagBlocksLowerTriangular" | custom-call | tf_op jit(solution)/shard_map/cholesky/custom-call.7 | solution.py:10
  697.8 11.7 %custom-call.34 = f32[128,128]{1,0:T(8,128)S(1)} custom-call(f32[128,128]{1,0:T(8,128)S(1)} %convolution_subtract_fusion.4), custom_call_target="Cholesky" | custom-call | tf_op jit(solution)/shard_map/cholesky/custom-call.3 | solution.py:10
  716.0 19.9 %custom-call.21 = f32[2,128,128]{1,2,0:T(8,128)S(1)} custom-call(f32[2,128,128]{2,1,0:T(8,128)S(1)} %get-tuple-element.124), custom_call_target="InvertDiagBlocksLowerTriangular" | custom-call | tf_op jit(solution)/shard_map/triangular_solve | solution.py:11
  (429 shorter events, 373.8 us)
Async XLA Ops:
  7.2 20.8 %copy-start.5 = (f32[512,256]{1,0:T(8,128)S(1)}, f32[512,256]{1,0:T(8,128)}, u32[]{:S(2)}) copy-start(f32[512,256]{1,0:T(8,128)} %param.17) | copy-start | bytes 1572868
  7.2 29.6 %all-gather.2.cloned.1.call-start = ((), (), s32[]{:S(2)}) async-start(), calls=%async_computation.1 | async-start | bytes 1310720 | tf_op jit(solution)/shard_map/all_gather | solution.py:93
  9.1 280.2 %all-reduce.9.cloned.1.call-start = ((), (), s32[]{:S(2)}) async-start(), calls=%async_computation.4 | async-start | bytes 5242880 | tf_op jit(solution)/shard_map/psum | solution.py:103
  177.8 1.5 copy-start.8
  177.8 1.5 copy-start.9
  179.3 155.0 %all-reduce.11.cloned.1.call-start = ((), (), s32[]{:S(2)}) async-start(), calls=%async_computation.5 | async-start | bytes 1048576 | tf_op jit(solution)/shard_map/psum | solution.py:82
  289.3 160.6 %all-reduce.7.cloned.1.call-start = ((), (), s32[]{:S(2)}) async-start(), calls=%async_computation.2 | async-start | bytes 524288 | tf_op jit(solution)/shard_map/psum | solution.py:105
  335.4 60.9 %copy-start.6 = (f32[2048,256]{1,0:T(8,128)S(1)}, f32[2048,256]{1,0:T(8,128)}, u32[]{:S(2)}) copy-start(f32[2048,256]{1,0:T(8,128)} %get-tuple-element.245) | copy-start | bytes 6291460
  376.6 21.7 %copy-start.10 = (s32[2,2]{1,0:T(2,128)}, s32[2,2]{1,0:T(2,128)S(1)}, u32[]{:S(2)}) copy-start(s32[2,2]{1,0:T(2,128)S(1)} %get-tuple-element.584) | copy-start | bytes 52
  400.2 52.3 %copy-start = (f32[2048,128]{1,0:T(8,128)}, f32[2048,128]{1,0:T(8,128)S(1)}, u32[]{:S(2)}) copy-start(f32[2048,128]{1,0:T(8,128)S(1)} %fusion.48) | copy-start | bytes 3145732
  402.2 1.0 copy-start.2
  407.5 328.5 %reduce-scatter.2.cloned.1.call-start = ((), (), s32[]{:S(2)}) async-start(), calls=%async_computation.3 | async-start | bytes 2621440 | tf_op jit(solution)/shard_map/reduce_scatter | solution.py:114
  672.9 1.2 copy-start.1
  672.9 1.5 copy-start.3
  672.9 2.2 copy-start.4
  672.9 2.2 copy-start.7
  675.3 36.8 %copy-start.11 = (s32[2,2]{1,0:T(2,128)S(1)}, s32[2,2]{1,0:T(2,128)}, u32[]{:S(2)}) copy-start(s32[2,2]{1,0:T(2,128)} %copy-done.10) | copy-start | bytes 52
Sparse Core Ops, SparseCore 0:
  10.2 26.4 all-gather.1
  179.5 109.7 all-reduce.8
  291.7 42.5 all-reduce.10
  407.6 42.2 all-reduce.6
  673.0 30.1 reduce-scatter.1
